TPU v7x, 32 devices: a whole 2x2x4 slice. The times are simulated.
32 devices in a mesh: dp: 4 (over z), ctx: 8 (over y, x, core).
Axes of the slice: x: 2, y: 2, z: 4, core: 2. Of those that a mesh axis runs over, the one named last changes fastest.
Arguments:
- queries: bfloat16 [4, 4096, 1024], P('dp', 'ctx'), may hold values from -6 to 6
- key_vectors: bfloat16 [4, 4096, 1024], P('dp', 'ctx'), may hold values from -6 to 6
- value_vectors: bfloat16 [4, 4096, 1024], P('dp', 'ctx'), may hold values from -6 to 6
- out_grad: bfloat16 [4, 4096, 1024], P('dp', 'ctx'), may hold values from -6 to 6
- column_bias: float32 [8], replicated, may hold values from -1 to 2
- column_offsets: int32 [1], replicated, may hold values from 0 to 63
Outputs:
- attended: bfloat16 [4, 4096, 1024], P('dp', 'ctx')
- query_grad: bfloat16 [4, 4096, 1024], P('dp', 'ctx')
- key_grad: bfloat16 [4, 4096, 1024], P('dp', 'ctx')
- value_grad: bfloat16 [4, 4096, 1024], P('dp', 'ctx')
- bias_grad: float32 [8], replicated
All inputs are finite; a program needn't handle non-finite values.
Results may differ from a plain program's by a relative error of at most 0.005.
The roundings to bfloat16 on the way count: a program that leaves them out, or rounds other values in their place, can miss the bound.
Values may be sent and summed in bfloat16 or wider, within the bound.
A program may use at most 128 MiB of HBM per device.

v0:
```python
import jax
import jax.numpy as jnp
from jax import lax
from jax.sharding import PartitionSpec as P

HEADS = 8
HEAD_DIM = 128
LOCAL_BAND = 512
STRIDE = 4096
CB = 64
TOKENS_PER_SHARD = 512


def from_behind(value, axis, by):
    size = lax.axis_size(axis)
    pairs = [(i, i + by) for i in range(size) if 0 <= i + by < size]
    return lax.ppermute(value, axis, pairs)


def column_flags(positions, offsets):
    window = positions // STRIDE
    within = positions % STRIDE
    picks = window[:, None] == jnp.arange(offsets.shape[0], dtype=jnp.int32)[None, :]
    offset_at = jnp.sum(jnp.where(picks, offsets[None, :], 0), axis=1)
    return (positions >= 0) & (within // CB == offset_at)


def head_block(qh, kb, vb, kc, vc, doh, bias_h, band_ok, band_col, col_ok):
    scale = HEAD_DIM ** (-0.5)
    sb = (
        jnp.dot(qh, kb.T, preferred_element_type=jnp.float32) * scale
        + jnp.where(band_col, bias_h, 0.0)[None, :]
    )
    sc = jnp.dot(qh, kc.T, preferred_element_type=jnp.float32) * scale + bias_h
    sb = jnp.where(band_ok, sb, -jnp.inf)
    sc = jnp.where(col_ok, sc, -jnp.inf)
    top = jnp.maximum(jnp.max(sb, axis=1), jnp.max(sc, axis=1))
    pb = jnp.exp(sb - top[:, None])
    pc = jnp.exp(sc - top[:, None])
    total = jnp.sum(pb, axis=1) + jnp.sum(pc, axis=1)
    wb = pb / total[:, None]
    wc = pc / total[:, None]
    wb16 = wb.astype(jnp.bfloat16)
    wc16 = wc.astype(jnp.bfloat16)
    mixed = jnp.dot(wb16, vb, preferred_element_type=jnp.float32) + jnp.dot(
        wc16, vc, preferred_element_type=jnp.float32
    )
    oh = mixed.astype(jnp.bfloat16)
    delta = jnp.sum(doh.astype(jnp.float32) * oh.astype(jnp.float32), axis=1)
    dsb = wb * (jnp.dot(doh, vb.T, preferred_element_type=jnp.float32) - delta[:, None])
    dsc = wc * (jnp.dot(doh, vc.T, preferred_element_type=jnp.float32) - delta[:, None])
    dbias = jnp.sum(jnp.where(band_col[None, :], dsb, 0.0)) + jnp.sum(dsc)
    dsb16 = dsb.astype(jnp.bfloat16)
    dsc16 = dsc.astype(jnp.bfloat16)
    dq = (
        (
            jnp.dot(dsb16, kb, preferred_element_type=jnp.float32)
            + jnp.dot(dsc16, kc, preferred_element_type=jnp.float32)
        )
        * scale
    ).astype(jnp.bfloat16)
    dkb = jnp.dot(dsb16.T, qh, preferred_element_type=jnp.float32) * scale
    dvb = jnp.dot(wb16.T, doh, preferred_element_type=jnp.float32)
    dkc = jnp.dot(dsc16.T, qh, preferred_element_type=jnp.float32) * scale
    dvc = jnp.dot(wc16.T, doh, preferred_element_type=jnp.float32)
    return (oh, dq, dkb, dvb, dkc, dvc, dbias, top, total, delta)


def separate_heads(x):
    return x.reshape(x.shape[0], HEADS, HEAD_DIM).transpose(1, 0, 2)


def join_heads(x):
    return x.transpose(1, 0, 2).reshape(x.shape[1], HEADS * HEAD_DIM)


def per_device(queries, key_vectors, value_vectors, out_grad, column_bias, column_offsets):
    here = lax.axis_index("ctx")
    count = lax.axis_size("ctx")
    start_position = here * TOKENS_PER_SHARD
    width = queries.shape[2]
    query_rows = queries[0]
    key_rows = key_vectors[0]
    value_rows = value_vectors[0]
    grad_rows = out_grad[0]
    ncol = column_offsets.shape[0]
    block_starts = jnp.arange(ncol, dtype=jnp.int32) * STRIDE + column_offsets * CB
    colpos = jnp.repeat(block_starts, CB) + jnp.tile(jnp.arange(CB, dtype=jnp.int32), ncol)
    window = start_position // STRIDE
    own_start = window * STRIDE + column_offsets[window] * CB
    local = jnp.clip(own_start - start_position, 0, TOKENS_PER_SHARD - CB)
    piece_k = lax.dynamic_slice_in_dim(key_rows, local, CB, 0)
    piece_v = lax.dynamic_slice_in_dim(value_rows, local, CB, 0)
    pieces_k, pieces_v = (
        lax.all_gather(piece_k, "ctx", axis=0, tiled=True),
        lax.all_gather(piece_v, "ctx", axis=0, tiled=True),
    )
    owner = block_starts // TOKENS_PER_SHARD
    col_k = pieces_k.reshape(count, CB, width)[owner].reshape(ncol * CB, width)
    col_v = pieces_v.reshape(count, CB, width)[owner].reshape(ncol * CB, width)
    prev_k, prev_v = from_behind((key_rows, value_rows), "ctx", 1)
    band_k = jnp.concatenate([prev_k, key_rows], axis=0)
    band_v = jnp.concatenate([prev_v, value_rows], axis=0)
    qpos = start_position + jnp.arange(TOKENS_PER_SHARD, dtype=jnp.int32)
    kpos = start_position - LOCAL_BAND + jnp.arange(LOCAL_BAND + TOKENS_PER_SHARD, dtype=jnp.int32)
    gap = qpos[:, None] - kpos[None, :]
    band_ok = (kpos[None, :] >= 0) & (gap >= 0) & (gap < LOCAL_BAND)
    band_col = column_flags(kpos, column_offsets)
    col_ok = colpos[None, :] <= qpos[:, None] - LOCAL_BAND

    def per_head(items):
        return head_block(
            items[0],
            items[1],
            items[2],
            items[3],
            items[4],
            items[5],
            items[6],
            band_ok,
            band_col,
            col_ok,
        )

    results = lax.map(
        per_head,
        (
            separate_heads(query_rows),
            separate_heads(band_k),
            separate_heads(band_v),
            separate_heads(col_k),
            separate_heads(col_v),
            separate_heads(grad_rows),
            column_bias,
        ),
    )
    oh, dq, dkb, dvb, dkc, dvc, dbias, top, total, delta = results
    attended = join_heads(oh)
    query_grad = join_heads(dq)
    dk_band = join_heads(dkb)
    dv_band = join_heads(dvb)
    own_dk = dk_band[dk_band.shape[0] - TOKENS_PER_SHARD :]
    own_dv = dv_band[dv_band.shape[0] - TOKENS_PER_SHARD :]
    back_k, back_v = from_behind((dk_band[:LOCAL_BAND], dv_band[:LOCAL_BAND]), "ctx", -1)
    own_dk = own_dk.at[TOKENS_PER_SHARD - LOCAL_BAND :].add(back_k)
    own_dv = own_dv.at[TOKENS_PER_SHARD - LOCAL_BAND :].add(back_v)
    summed_k, summed_v = lax.psum((join_heads(dkc), join_heads(dvc)), "ctx")
    flags = column_flags(qpos, column_offsets)
    source = jnp.clip(qpos // STRIDE * CB + qpos % CB, 0, ncol * CB - 1)
    own_dk = own_dk + jnp.where(flags[:, None], summed_k[source], 0.0)
    own_dv = own_dv + jnp.where(flags[:, None], summed_v[source], 0.0)
    bias_grad = lax.psum(dbias, ("dp", "ctx"))
    return (
        attended[None],
        query_grad[None],
        own_dk.astype(jnp.bfloat16)[None],
        own_dv.astype(jnp.bfloat16)[None],
        bias_grad,
    )


def solution(mesh):
    placed = (
        P("dp", "ctx", None),
        P("dp", "ctx", None),
        P("dp", "ctx", None),
        P("dp", "ctx", None),
        P(),
        P(),
    )
    return jax.shard_map(
        per_device,
        mesh=mesh,
        in_specs=placed,
        out_specs=(
            P("dp", "ctx", None),
            P("dp", "ctx", None),
            P("dp", "ctx", None),
            P("dp", "ctx", None),
            P(),
        ),
        check_vma=False,
    )
```

profile of v0, /device:TPU:0, one launch (start us, length us, event | category | flops | bytes accessed | tf_op | source)
XLA Modules:
  0.0 354.4 jit_solution(14615889557479074196)
XLA Ops:
  12.8 3.3 collective-permute-start
  16.7 4.5 %collective-permute-start.1 = (bf16[512,1024]{0,1:T(8,128)(2,1)S(1)}, bf16[512,1024]{0,1:T(8,128)(2,1)}, u32[]{:S(2)}, u32[]{:S(2)}) collective-permute-start(bf16[512,1024]{0,1:T(8,128)(2,1)S(1)} %bitcast.242), channel_id=1, source_target_pairs={{0,1},{1,2},{2,3},{3,4},{4,5},{5,6},{6,7},{8,9},{9,10},{10,11},{11... | collective-permute-start | bytes 3145736 | tf_op jit(solution)/shard_map/ppermute | solution.py:17
  22.7 2.3 copy.26
  25.1 2.9 maximum_bitcast_fusion
  28.0 2.9 maximum_bitcast_fusion.1
  30.9 7.3 %all-gather.7.cloned.1.call-done = bf16[1,512,1024]{2,1,0:T(8,128)(2,1)} async-done(((bf16[1,64,1024]{2,1,0:T(8,128)(2,1)}), bf16[1,512,1024]{2,1,0:T(8,128)(2,1)}) %all-gather.7.cloned.1.call-update) | async-done | bytes 1048592 | tf_op jit(solution)/shard_map/all_gather | solution.py:96
  38.2 25.5 %all-gather.5.cloned.1.call-done = bf16[1,512,1024]{2,1,0:T(8,128)(2,1)} async-done(((bf16[1,64,1024]{2,1,0:T(8,128)(2,1)}), bf16[1,512,1024]{2,1,0:T(8,128)(2,1)}) %all-gather.5.cloned.1.call-update) | async-done | bytes 1048592 | tf_op jit(solution)/shard_map/all_gather | solution.py:95
  65.4 169.8 %while.29 = (s32[]{:T(128)}, bf16[8,512,128]{1,2,0:T(8,128)(2,1)}, bf16[8,512,128]{2,1,0:T(8,128)(2,1)}, f32[8,1024,128]{2,1,0:T(8,128)}, f32[8,1024,128]{2,1,0:...) while((s32[]{:T(128)}, bf16[8,512,128]{1,2,0:T(8,128)(2,1)}, ...), condition=%wide.region_8.9_spmd.clone, body=%wide.region_0.8_spmd.clone.sunk | while | flops 869654016 | bytes 19551504 | solution.py:125
  67.3 2.0 fusion.160
  72.3 1.6 fusion.164
  73.9 1.6 bitcast_dynamic-update-slice_fusion.2
  77.8 2.5 select_reduce_fusion.2
  88.6 2.0 fusion.160
  93.5 1.6 fusion.164
  95.1 1.6 bitcast_dynamic-update-slice_fusion.2
  99.0 2.5 select_reduce_fusion.2
  109.8 2.0 fusion.160
  113.2 1.6 fusion.170
  114.8 1.6 fusion.164
  116.4 1.6 bitcast_dynamic-update-slice_fusion.2
  120.2 2.5 select_reduce_fusion.2
  131.0 2.0 fusion.160
  136.0 1.6 fusion.164
  137.6 1.6 bitcast_dynamic-update-slice_fusion.2
  141.4 2.5 select_reduce_fusion.2
  152.2 2.0 fusion.160
  157.2 1.6 fusion.164
  158.8 1.6 bitcast_dynamic-update-slice_fusion.2
  162.7 2.5 select_reduce_fusion.2
  173.5 2.0 fusion.160
  178.4 1.6 fusion.164
  183.9 2.5 select_reduce_fusion.2
  194.7 2.0 fusion.160
  199.6 1.6 fusion.164
  201.3 1.6 bitcast_dynamic-update-slice_fusion.2
  205.1 2.5 select_reduce_fusion.2
  215.9 2.0 fusion.160
  219.3 1.6 fusion.170
  220.9 1.6 fusion.164
  226.4 2.5 select_reduce_fusion.2
  235.3 4.0 %slice_bitcast_fusion.3 = (f32[8,64,8,128]{3,2,1,0:T(8,128)}, f32[8,64,8,128]{3,2,1,0:T(8,128)S(1)}) fusion(f32[1024,8,128]{2,0,1:T(8,128)} %bitcast.240), kind=kLoop, calls=%fused_computation.130 | loop fusion | bytes 8388608
  242.3 1.6 slice_bitcast_fusion.1
  243.9 1.6 copy.63
  248.4 79.4 %psum.23 = f32[8]{0:T(128)} all-reduce(f32[8]{0:T(128)S(1)} %get-tuple-element.149), channel_id=1, replica_groups=mesh['dp'=4,'ctx'=8] {'dp','ctx'}, use_global_device_ids=true, to_apply=%region_11.12 | all-reduce | flops 8 | bytes 64 | tf_op jit(solution)/shard_map/psum | solution.py:152
  331.1 4.3 %all-reduce.3.cloned.1.call-done = (f32[64,1024]{1,0:T(8,128)}, f32[64,1024]{1,0:T(8,128)}) async-done(((f32[64,1024]{1,0:T(8,128)}, f32[64,1024]{1,0:T(8,128)}), (f32[64,1024]{1,0:T(8,128)}, f32[64,1024]{1,0:T(8,128)})) %all-reduce.3.cloned.1.call-update) | async-done | bytes 524304 | tf_op jit(solution)/shard_map/psum | solution.py:147
  335.3 3.8 %gather_fusion = f32[512,1024]{1,0:T(8,128)S(1)} fusion(f32[64,1024]{1,0:T(8,128)} %get-tuple-element.315, s32[1024]{0:T(1024)S(1)} %pad_clamp_fusion), kind=kCustom, calls=%fused_computation | custom fusion | bytes 4196352 | tf_op jit(solution)/shard_map/gather | solution.py:150
  339.2 2.7 gather_fusion.1
  341.8 6.0 %fusion.99 = (bf16[1,512,1024]{2,1,0:T(8,128)(2,1)}, bf16[1,512,1024]{2,1,0:T(8,128)(2,1)}) fusion(f32[512,1024]{1,0:T(8,128)} %gather_fusion.1, f32[512,1024]{1,0:T(8,128)} %collective-permute-done.3, f32[8,64,8,128]{3,2,1,0:T(8,128)} %get-tuple-element.327, pred[512]{0:T(512)(128)(4,1)S(1)} %fusion.108, f32[512,1024]{1,0:T(8,128)S(1)} %gather_fusion, ...), kind=kLoop, calls=%fused_computation.134 | loop fusion | flops 4194304 | bytes 14680576 | tf_op jit(solution)/shard_map/convert_element_type | solution.py:157
  (196 shorter events, 116.1 us)
Async XLA Ops:
  7.2 9.0 %copy-start.3 = (bf16[1,512,1024]{2,1,0:T(8,128)(2,1)S(1)}, bf16[1,512,1024]{2,1,0:T(8,128)(2,1)}, u32[]{:S(2)}) copy-start(bf16[1,512,1024]{2,1,0:T(8,128)(2,1)} %param.18) | copy-start | bytes 3145732
  7.2 31.1 %all-gather.7.cloned.1.call-start = ((), (), s32[]{:S(2)}) async-start(), calls=%async_computation.1 | async-start | bytes 1179648 | tf_op jit(solution)/shard_map/all_gather | solution.py:96
  9.6 54.1 %all-gather.5.cloned.1.call-start = ((), (), s32[]{:S(2)}) async-start(), calls=%async_computation | async-start | bytes 1179648 | tf_op jit(solution)/shard_map/all_gather | solution.py:95
  11.2 324.1 %all-reduce.3.cloned.1.call-start = ((), (), s32[]{:S(2)}) async-start(), calls=%async_computation.2 | async-start | bytes 1048576 | tf_op jit(solution)/shard_map/psum | solution.py:147
  12.8 12.3 %collective-permute-start = (bf16[512,1024]{0,1:T(8,128)(2,1)S(1)}, bf16[512,1024]{0,1:T(8,128)(2,1)}, u32[]{:S(2)}, u32[]{:S(2)}) collective-permute-start(bf16[512,1024]{0,1:T(8,128)(2,1)S(1)} %bitcast.244), channel_id=1, source_target_pairs={{0,1},{1,2},{2,3},{3,4},{4,5},{5,6},{6,7},{8,9},{9,10},{10,11},{11... | collective-permute-start | bytes 3145736 | tf_op jit(solution)/shard_map/ppermute | solution.py:17
  16.7 11.3 %collective-permute-start.1 = (bf16[512,1024]{0,1:T(8,128)(2,1)S(1)}, bf16[512,1024]{0,1:T(8,128)(2,1)}, u32[]{:S(2)}, u32[]{:S(2)}) collective-permute-start(bf16[512,1024]{0,1:T(8,128)(2,1)S(1)} %bitcast.242), channel_id=1, source_target_pairs={{0,1},{1,2},{2,3},{3,4},{4,5},{5,6},{6,7},{8,9},{9,10},{10,11},{11... | collective-permute-start | bytes 3145736 | tf_op jit(solution)/shard_map/ppermute | solution.py:17
  28.0 37.5 %copy-start.2 = (bf16[1,512,1024]{1,2,0:T(8,128)(2,1)S(1)}, bf16[1,512,1024]{1,2,0:T(8,128)(2,1)}, u32[]{:S(2)}) copy-start(bf16[1,512,1024]{1,2,0:T(8,128)(2,1)} %copy.26) | copy-start | bytes 3145732
  28.0 37.5 %copy-start.8 = (f32[8]{0:T(128)S(1)}, f32[8]{0:T(128)}, u32[]{:S(2)}) copy-start(f32[8]{0:T(128)} %param.20) | copy-start | bytes 100
  239.2 3.0 copy-start.1
  240.8 101.0 %collective-permute-start.2 = (f32[512,1024]{1,0:T(8,128)}, f32[512,1024]{1,0:T(8,128)}, u32[]{:S(2)}, u32[]{:S(2)}) collective-permute-start(f32[512,1024]{1,0:T(8,128)} %bitcast.178), channel_id=1, source_target_pairs={{1,0},{2,1},{3,2},{4,3},{5,4},{6,5},{7,6},{9,8},{10,9},{11,10},{12... | collective-permute-start | bytes 6291464 | tf_op jit(solution)/shard_map/ppermute | solution.py:17
  243.9 2.9 copy-start.7
  243.9 3.7 %copy-start.6 = (f32[8,64,128]{2,1,0:T(8,128)S(1)}, f32[8,64,128]{2,1,0:T(8,128)}, u32[]{:S(2)}) copy-start(f32[8,64,128]{2,1,0:T(8,128)} %get-tuple-element.146) | copy-start | bytes 786436
  243.9 83.9 %copy-start.5 = (bf16[8,512,128]{2,1,0:T(8,128)(2,1)S(1)}, bf16[8,512,128]{2,1,0:T(8,128)(2,1)}, u32[]{:S(2)}) copy-start(bf16[8,512,128]{2,1,0:T(8,128)(2,1)} %get-tuple-element.144) | copy-start | bytes 3145732
  245.5 96.3 %collective-permute-start.3 = (f32[512,1024]{1,0:T(8,128)}, f32[512,1024]{1,0:T(8,128)}, u32[]{:S(2)}, u32[]{:S(2)}) collective-permute-start(f32[512,1024]{1,0:T(8,128)} %bitcast.177), channel_id=1, source_target_pairs={{1,0},{2,1},{3,2},{4,3},{5,4},{6,5},{7,6},{9,8},{10,9},{11,10},{12... | collective-permute-start | bytes 6291464 | tf_op jit(solution)/shard_map/ppermute | solution.py:17
  327.8 2.0 copy-start.4
  335.3 3.8 %copy-start = (f32[64,1024]{1,0:T(8,128)S(1)}, f32[64,1024]{1,0:T(8,128)}, u32[]{:S(2)}) copy-start(f32[64,1024]{1,0:T(8,128)} %get-tuple-element.316) | copy-start | bytes 786436
Sparse Core Ops, SparseCore 0:
  9.9 28.2 all-gather.6
  40.1 23.5 all-gather.4
  248.4 86.8 all-reduce.2
where the time goes:
time: 357 us; the launch traced here: 354 us
  matrix products  133 us (37%)
  blocking collectives  79.4 us (22%)
  waiting for transfers between devices  37.1 us (10%)
  local copies, waits for them, and re-layouts  36.4 us (10%)
  other arithmetic  32.7 us (9%)
  between operations  14.7 us (4%)
  starting transfers between devices  10.7 us (3%)
  loops' own time  10 us (3%)
    psum x1, blocking collectives, per_device(): bias_grad = lax.psum(dbias, ('dp', 'ctx'))  79.4 us
    all_gather x1, waiting for transfers between devices, per_device(): lax.all_gather(piece_k, 'ctx', axis=0, tiled=True)  25.5 us
    dot_general x8, matrix products, head_block(): jnp.dot(doh, vb.T, preferred_element_type=jnp.float32) - delta[:, None]  19.7 us
    dot_general x8, matrix products, head_block(): jnp.dot(qh, kb.T, preferred_element_type=jnp.float32) * scale  15.9 us
    unnamed x29, local copies, waits for them, and re-layouts  13.2 us
    dot_general x8, matrix products, head_block(): jnp.dot(wb16, vb, preferred_element_type=jnp.float32)  12.9 us
    dot_general x8, matrix products, head_block(): jnp.dot(wc16, vc, preferred_element_type=jnp.float32)  12.9 us
    dot_general x8, matrix products, head_block(): dvb = jnp.dot(wb16.T, doh, preferred_element_type=jnp.float32)  12.7 us
  transfers between devices with their start and end apart: 7, of which 3 were waited for; matrix products, arithmetic and copies ran while one was open for 8% of the time, Pallas kernels for 0%

commit v1 on v0

--- a/solution.py
+++ b/solution.py
@@ -9,6 +9,18 @@
 STRIDE = 4096
 CB = 64
 TOKENS_PER_SHARD = 512
+
+
+def doubled_up(value, axis, dim):
+    ways, here, hop = (lax.axis_size(axis), lax.axis_index(axis), value.shape[dim])
+    line, have = (value, 1)
+    while have < ways:
+        line = jnp.concatenate(
+            [line, lax.ppermute(line, axis, [(d, (d - have) % ways) for d in range(ways)])],
+            axis=dim,
+        )
+        have = 2 * have
+    return jnp.roll(line, here * hop, axis=dim)
 
 
 def from_behind(value, axis, by):
@@ -92,7 +104,7 @@
     piece_k = lax.dynamic_slice_in_dim(key_rows, local, CB, 0)
     piece_v = lax.dynamic_slice_in_dim(value_rows, local, CB, 0)
     pieces_k, pieces_v = (
-        lax.all_gather(piece_k, "ctx", axis=0, tiled=True),
+        doubled_up(piece_k, "ctx", 0),
         lax.all_gather(piece_v, "ctx", axis=0, tiled=True),
     )
     owner = block_starts // TOKENS_PER_SHARD

time: 357 us -> 368 us (1.031)
  local copies, waits for them, and re-layouts: 36.4 us -> 45.3 us
  waiting for transfers between devices: 37.1 us -> 31.9 us
    ppermute x0 -> x3, waiting for transfers between devices: none -> 28.8 us  [doubled_up(): lax.ppermute(line, axis, [(d, (d - have) % ways) for d in range(ways)])]
    all_gather x1 -> x0, waiting for transfers between devices: 25.5 us -> none  [per_device(): lax.all_gather(piece_k, 'ctx', axis=0, tiled=True)]
    unnamed x29 -> x44, local copies, waits for them, and re-layouts: 13.2 us -> 20.6 us
    all_gather x1, waiting for transfers between devices: 7.35 us -> 0.01 us  [per_device(): lax.all_gather(piece_v, 'ctx', axis=0, tiled=True)]
    ppermute x0 -> x3, starting transfers between devices: none -> 3.97 us  [doubled_up(): lax.ppermute(line, axis, [(d, (d - have) % ways) for d in range(ways)])]
  transfers between devices with their start and end apart: 7 -> 9, of which waited for: 3 -> 3; matrix products, arithmetic and copies ran while one was open for 8% -> 10% of each run, Pallas kernels for 0% -> 0%
where the time goes in v1:
time: 368 us; the launch traced here: 365 us
  matrix products  133 us (36%)
  blocking collectives  80.6 us (22%)
  local copies, waits for them, and re-layouts  45.3 us (12%)
  other arithmetic  34.9 us (9%)
  waiting for transfers between devices  31.9 us (9%)
  between operations  15 us (4%)
  starting transfers between devices  14.3 us (4%)
  loops' own time  10 us (3%)
    psum x1, blocking collectives, per_device(): bias_grad = lax.psum(dbias, ('dp', 'ctx'))  80.6 us
    ppermute x3, waiting for transfers between devices, doubled_up(): lax.ppermute(line, axis, [(d, (d - have) % ways) for d in range(ways)])  28.8 us
    unnamed x44, local copies, waits for them, and re-layouts  20.6 us
    dot_general x8, matrix products, head_block(): jnp.dot(doh, vb.T, preferred_element_type=jnp.float32) - delta[:, None]  19.7 us
    dot_general x8, matrix products, head_block(): jnp.dot(qh, kb.T, preferred_element_type=jnp.float32) * scale  15.9 us
    dot_general x8, matrix products, head_block(): jnp.dot(wb16, vb, preferred_element_type=jnp.float32)  12.9 us
    dot_general x8, matrix products, head_block(): jnp.dot(wc16, vc, preferred_element_type=jnp.float32)  12.9 us
    dot_general x8, matrix products, head_block(): dvb = jnp.dot(wb16.T, doh, preferred_element_type=jnp.float32)  12.7 us
  transfers between devices with their start and end apart: 9, of which 3 were waited for; matrix products, arithmetic and copies ran while one was open for 10% of the time, Pallas kernels for 0%

profile of v1, /device:TPU:0, one launch (start us, length us, event | category | flops | bytes accessed | tf_op | source)
XLA Modules:
  0.0 365.2 jit_solution(11314886545845575888)
XLA Ops:
  8.0 1.6 constant_dynamic-update-slice_fusion.7
  9.6 3.3 collective-permute-start.1
  12.9 2.5 collective-permute-done.1
  20.5 5.2 %collective-permute-start = (bf16[512,1024]{0,1:T(8,128)(2,1)S(1)}, bf16[512,1024]{0,1:T(8,128)(2,1)}, u32[]{:S(2)}, u32[]{:S(2)}) collective-permute-start(bf16[512,1024]{0,1:T(8,128)(2,1)S(1)} %bitcast.247), channel_id=1, source_target_pairs={{0,1},{1,2},{2,3},{3,4},{4,5},{5,6},{6,7},{8,9},{9,10},{10,11},{11... | collective-permute-start | bytes 3145736 | tf_op jit(solution)/shard_map/ppermute | solution.py:29
  26.3 2.3 collective-permute-start.4
  30.1 2.3 copy.26
  36.3 26.3 %collective-permute-done.3 = bf16[256,1024]{1,0:T(8,128)(2,1)S(1)} collective-permute-done((bf16[256,1024]{1,0:T(8,128)(2,1)S(1)}, bf16[256,1024]{1,0:T(8,128)(2,1)S(1)}, u32[]{:S(2)}, u32[]{:S(2)}) %collective-permute-start.3) | collective-permute-done | bytes 524320 | tf_op jit(solution)/shard_map/ppermute | solution.py:19
  66.4 2.3 constant_dynamic-slice_fusion.1
  68.6 2.9 maximum_bitcast_fusion
  71.5 2.9 maximum_bitcast_fusion.1
  76.2 169.6 %while.29 = (s32[]{:T(128)}, bf16[8,512,128]{1,2,0:T(8,128)(2,1)}, bf16[8,512,128]{2,1,0:T(8,128)(2,1)}, f32[8,1024,128]{2,1,0:T(8,128)}, f32[8,1024,128]{2,1,0:...) while((s32[]{:T(128)}, bf16[8,512,128]{1,2,0:T(8,128)(2,1)}, ...), condition=%wide.region_8.9_spmd.clone, body=%wide.region_0.8_spmd.clone.sunk | while | flops 869654016 | bytes 19551504 | solution.py:137
  78.1 2.0 fusion.160
  83.1 1.6 fusion.164
  88.5 2.5 select_reduce_fusion.2
  99.3 2.0 fusion.160
  104.3 1.6 fusion.164
  105.9 1.6 bitcast_dynamic-update-slice_fusion.2
  109.7 2.5 select_reduce_fusion.2
  120.5 2.0 fusion.160
  123.9 1.6 fusion.170
  125.5 1.6 fusion.164
  127.1 1.6 bitcast_dynamic-update-slice_fusion.2
  131.0 2.5 select_reduce_fusion.2
  141.8 2.0 fusion.160
  146.7 1.6 fusion.164
  152.2 2.5 select_reduce_fusion.2
  163.0 2.0 fusion.160
  167.9 1.6 fusion.164
  173.4 2.5 select_reduce_fusion.2
  184.2 2.0 fusion.160
  189.1 1.6 fusion.164
  194.6 2.5 select_reduce_fusion.2
  205.3 2.0 fusion.160
  210.3 1.6 fusion.164
  215.8 2.5 select_reduce_fusion.2
  226.5 2.0 fusion.160
  229.9 1.6 fusion.170
  231.5 1.6 fusion.164
  237.0 2.5 select_reduce_fusion.2
  245.9 4.0 %slice_bitcast_fusion.3 = (f32[8,64,8,128]{3,2,1,0:T(8,128)}, f32[8,64,8,128]{3,2,1,0:T(8,128)S(1)}) fusion(f32[1024,8,128]{2,0,1:T(8,128)} %bitcast.243), kind=kLoop, calls=%fused_computation.130 | loop fusion | bytes 8388608
  249.8 1.6 copy.64
  252.9 1.6 slice_bitcast_fusion.1
  254.5 1.6 copy.63
  259.0 80.6 %psum.23 = f32[8]{0:T(128)} all-reduce(f32[8]{0:T(128)S(1)} %get-tuple-element.149), channel_id=1, replica_groups=mesh['dp'=4,'ctx'=8] {'dp','ctx'}, use_global_device_ids=true, to_apply=%region_11.12 | all-reduce | flops 8 | bytes 64 | tf_op jit(solution)/shard_map/psum | solution.py:164
  342.8 3.0 all-reduce.3.cloned.1.call-done
  345.8 3.8 %gather_fusion = f32[512,1024]{1,0:T(8,128)S(1)} fusion(f32[64,1024]{1,0:T(8,128)} %get-tuple-element.315, s32[1024]{0:T(1024)S(1)} %pad_clamp_fusion), kind=kCustom, calls=%fused_computation | custom fusion | bytes 4196352 | tf_op jit(solution)/shard_map/gather | solution.py:162
  349.7 2.7 gather_fusion.1
  352.3 6.0 %fusion.99 = (bf16[1,512,1024]{2,1,0:T(8,128)(2,1)}, bf16[1,512,1024]{2,1,0:T(8,128)(2,1)}) fusion(f32[512,1024]{1,0:T(8,128)} %gather_fusion.1, f32[512,1024]{1,0:T(8,128)} %collective-permute-done.6, f32[8,64,8,128]{3,2,1,0:T(8,128)} %get-tuple-element.329, pred[512]{0:T(512)(128)(4,1)S(1)} %fusion.108, f32[512,1024]{1,0:T(8,128)S(1)} %gather_fusion, ...), kind=kLoop, calls=%fused_computation.134 | loop fusion | flops 4194304 | bytes 14680576 | tf_op jit(solution)/shard_map/convert_element_type | solution.py:169
  (217 shorter events, 128.7 us)
Async XLA Ops:
  7.2 18.6 %copy-start.5 = (bf16[1,512,1024]{2,1,0:T(8,128)(2,1)S(1)}, bf16[1,512,1024]{2,1,0:T(8,128)(2,1)}, u32[]{:S(2)}) copy-start(bf16[1,512,1024]{2,1,0:T(8,128)(2,1)} %param.18) | copy-start | bytes 3145732
  7.2 67.3 %all-gather.3.cloned.1.call-start = ((), (), s32[]{:S(2)}) async-start(), calls=%async_computation | async-start | bytes 1179648 | tf_op jit(solution)/shard_map/all_gather | solution.py:108
  9.6 5.9 %collective-permute-start.1 = (bf16[64,1024]{1,0:T(8,128)(2,1)S(1)}, bf16[64,1024]{1,0:T(8,128)(2,1)S(1)}, u32[]{:S(2)}, u32[]{:S(2)}) collective-permute-start(bf16[64,1024]{1,0:T(8,128)(2,1)S(1)} %get-tuple-element.318), channel_id=1, source_target_pairs={{0,7},{1,0},{2,1},{3,2},{4,3},{5,4},{6,5},{7,6},{8,15},{9,8},{10,9... | collective-permute-start | bytes 393224 | tf_op jit(solution)/shard_map/ppermute | solution.py:19
  15.4 0.6 copy-start.3
  16.8 15.6 %collective-permute-start.2 = (bf16[128,1024]{1,0:T(8,128)(2,1)}, bf16[128,1024]{1,0:T(8,128)(2,1)S(1)}, u32[]{:S(2)}, u32[]{:S(2)}) collective-permute-start(bf16[128,1024]{1,0:T(8,128)(2,1)} %pad_maximum_fusion.1), channel_id=1, source_target_pairs={{0,6},{1,7},{2,0},{3,1},{4,2},{5,3},{6,4},{7,5},{8,14},{9,15},{10,... | collective-permute-start | bytes 786440 | tf_op jit(solution)/shard_map/ppermute | solution.py:19
  19.0 326.9 %all-reduce.3.cloned.1.call-start = ((), (), s32[]{:S(2)}) async-start(), calls=%async_computation.1 | async-start | bytes 1048576 | tf_op jit(solution)/shard_map/psum | solution.py:159
  20.5 48.1 %collective-permute-start = (bf16[512,1024]{0,1:T(8,128)(2,1)S(1)}, bf16[512,1024]{0,1:T(8,128)(2,1)}, u32[]{:S(2)}, u32[]{:S(2)}) collective-permute-start(bf16[512,1024]{0,1:T(8,128)(2,1)S(1)} %bitcast.247), channel_id=1, source_target_pairs={{0,1},{1,2},{2,3},{3,4},{4,5},{5,6},{6,7},{8,9},{9,10},{10,11},{11... | collective-permute-start | bytes 3145736 | tf_op jit(solution)/shard_map/ppermute | solution.py:29
  26.3 45.2 %collective-permute-start.4 = (bf16[512,1024]{0,1:T(8,128)(2,1)S(1)}, bf16[512,1024]{0,1:T(8,128)(2,1)}, u32[]{:S(2)}, u32[]{:S(2)}) collective-permute-start(bf16[512,1024]{0,1:T(8,128)(2,1)S(1)} %bitcast.245), channel_id=1, source_target_pairs={{0,1},{1,2},{2,3},{3,4},{4,5},{5,6},{6,7},{8,9},{9,10},{10,11},{11... | collective-permute-start | bytes 3145736 | tf_op jit(solution)/shard_map/ppermute | solution.py:29
  32.4 31.8 %copy-start.4 = (bf16[64,1024]{1,0:T(8,128)(2,1)S(1)}, bf16[64,1024]{1,0:T(8,128)(2,1)}, u32[]{:S(2)}) copy-start(bf16[64,1024]{1,0:T(8,128)(2,1)} %copy-done.3) | copy-start | bytes 393220
  33.4 29.2 %collective-permute-start.3 = (bf16[256,1024]{1,0:T(8,128)(2,1)S(1)}, bf16[256,1024]{1,0:T(8,128)(2,1)S(1)}, u32[]{:S(2)}, u32[]{:S(2)}) collective-permute-start(bf16[256,1024]{1,0:T(8,128)(2,1)S(1)} %pad_maximum_fusion), channel_id=1, source_target_pairs={{0,4},{1,5},{2,6},{3,7},{4,0},{5,1},{6,2},{7,3},{8,12},{9,13},{10,... | collective-permute-start | bytes 1572872 | tf_op jit(solution)/shard_map/ppermute | solution.py:19
  71.5 4.7 %copy-start.2 = (bf16[1,512,1024]{1,2,0:T(8,128)(2,1)S(1)}, bf16[1,512,1024]{1,2,0:T(8,128)(2,1)}, u32[]{:S(2)}) copy-start(bf16[1,512,1024]{1,2,0:T(8,128)(2,1)} %copy.26) | copy-start | bytes 3145732
  71.5 4.7 %copy-start.10 = (f32[8]{0:T(128)S(1)}, f32[8]{0:T(128)}, u32[]{:S(2)}) copy-start(f32[8]{0:T(128)} %param.20) | copy-start | bytes 100
  71.5 4.7 %copy-start.11 = (pred[1024]{0:T(1024)(128)(4,1)S(1)}, pred[1024]{0:T(1024)(128)(4,1)}, u32[]{:S(2)}) copy-start(pred[1024]{0:T(1024)(128)(4,1)} %broadcast_compare_fusion) | copy-start | bytes 3076
  71.5 4.7 %copy-start.12 = (f32[8]{0:T(128)S(1)}, f32[8]{0:T(128)}, u32[]{:S(2)}) copy-start(f32[8]{0:T(128)} %custom-call.11) | copy-start | bytes 100
  249.8 3.0 copy-start.1
  251.4 100.9 %collective-permute-start.5 = (f32[512,1024]{1,0:T(8,128)}, f32[512,1024]{1,0:T(8,128)}, u32[]{:S(2)}, u32[]{:S(2)}) collective-permute-start(f32[512,1024]{1,0:T(8,128)} %bitcast.181), channel_id=1, source_target_pairs={{1,0},{2,1},{3,2},{4,3},{5,4},{6,5},{7,6},{9,8},{10,9},{11,10},{12... | collective-permute-start | bytes 6291464 | tf_op jit(solution)/shard_map/ppermute | solution.py:29
  254.5 2.9 copy-start.8
  254.5 3.7 %copy-start.9 = (f32[8,64,128]{2,1,0:T(8,128)S(1)}, f32[8,64,128]{2,1,0:T(8,128)}, u32[]{:S(2)}) copy-start(f32[8,64,128]{2,1,0:T(8,128)} %get-tuple-element.146) | copy-start | bytes 786436
  254.5 85.0 %copy-start.7 = (bf16[8,512,128]{2,1,0:T(8,128)(2,1)S(1)}, bf16[8,512,128]{2,1,0:T(8,128)(2,1)}, u32[]{:S(2)}) copy-start(bf16[8,512,128]{2,1,0:T(8,128)(2,1)} %get-tuple-element.144) | copy-start | bytes 3145732
  256.1 96.2 %collective-permute-start.6 = (f32[512,1024]{1,0:T(8,128)}, f32[512,1024]{1,0:T(8,128)}, u32[]{:S(2)}, u32[]{:S(2)}) collective-permute-start(f32[512,1024]{1,0:T(8,128)} %bitcast.180), channel_id=1, source_target_pairs={{1,0},{2,1},{3,2},{4,3},{5,4},{6,5},{7,6},{9,8},{10,9},{11,10},{12... | collective-permute-start | bytes 6291464 | tf_op jit(solution)/shard_map/ppermute | solution.py:29
  339.5 2.0 copy-start.6
  345.8 3.8 %copy-start = (f32[64,1024]{1,0:T(8,128)S(1)}, f32[64,1024]{1,0:T(8,128)}, u32[]{:S(2)}) copy-start(f32[64,1024]{1,0:T(8,128)} %get-tuple-element.316) | copy-start | bytes 786436
Sparse Core Ops, SparseCore 0:
  19.1 35.1 all-gather.2
  259.0 86.7 all-reduce.2
